TPU v7x, 256 devices: a whole 4x4x8 slice. The times are simulated.
256 devices in a mesh: expert: 32 (over x, y, core), shard: 8 (over z).
Axes of the slice: x: 4, y: 4, z: 8, core: 2. Of those that a mesh axis runs over, the one named last changes fastest.
Arguments:
- head_outputs: bfloat16 [32768, 1024], P(('expert', 'shard')), may hold values from -6 to 6
- residual: bfloat16 [32768, 1024], P(('expert', 'shard')), may hold values from -4 to 4
- output_weight: bfloat16 [1024, 1024], P('shard'), may hold values from -0.1875 to 0.1875
- router: bfloat16 [1024, 32], replicated, may hold values from -0.095703125 to 0.095703125
- norm_gain: float32 [1024], replicated, may hold values from 0.1 to 1.9
- placed_gate_up: bfloat16 [64, 1024, 1024], P('expert', 'shard'), may hold values from -0.1875 to 0.1875
- placed_down: bfloat16 [64, 512, 1024], P('expert', 'shard'), may hold values from -0.25 to 0.25
- routes: int32 [32768, 8], P(('expert', 'shard')), may hold values from 0 to 31, all different within a row; in each aligned block of 128 rows (0 to 127, 128 to 255, ...) at most 48 rows name the same one
- replica_pick: int32 [32768, 8], P(('expert', 'shard')), may hold values from 0 to 5
- placement: int32 [64], replicated, may hold values from 0 to 31, as said below
- final_gain: float32 [1024], replicated, may hold values from 0.1 to 1.9
Outputs:
- next_input: bfloat16 [32768, 1024], P(('expert', 'shard'))
Inputs may be any that keep to these rules, and one draw needn't show every extreme that they name: `routes`: each token names 8 different experts. Among the 128 tokens of one device no expert is named more than 48 times, and in some device's tokens one expert is named exactly 48 times. `placement`: every expert holds one to three of the 64 placements: a quarter of the experts hold three, half of them two, the rest one.
All inputs are finite; a program needn't handle non-finite values.
Results may differ from a plain program's by a relative error of at most 0.011.
Values may be sent and summed in bfloat16 or wider, within the bound.
A program may use at most 128 MiB of HBM per device.

v0:
```python
import math
import jax
import jax.numpy as jnp
from jax import lax
from jax.sharding import PartitionSpec as P

CAP = 48
eps_norm = 1e-06
most_copies = 3


def rms_scale(values, scale_gain):
    mean_square = jnp.mean(values * values, axis=-1, keepdims=True)
    return values * lax.rsqrt(mean_square + eps_norm) * scale_gain


def choose_slots(routes, replica_pick, placement, experts):
    labels = jnp.arange(experts, dtype=jnp.int32)
    holder_mask = (placement[None, :] == labels[:, None]).astype(jnp.int32)
    before = jnp.cumsum(holder_mask, axis=1) - holder_mask
    copies = jnp.sum(holder_mask, axis=1)
    places = jnp.arange(placement.shape[0], dtype=jnp.int32)
    route_hits = (routes[..., None] == labels).astype(jnp.int32)
    held_count = jnp.sum(route_hits * copies, axis=-1)
    wanted = replica_pick % held_count
    chosen = jnp.zeros(routes.shape, jnp.int32)
    for replica in range(most_copies):
        column = jnp.sum(
            holder_mask * (before == replica).astype(jnp.int32) * places[None, :], axis=1
        )
        candidate = jnp.sum(route_hits * column, axis=-1)
        chosen = jnp.where(wanted == replica, candidate, chosen)
    return chosen


def padded_experts(inbound, gate_up, down_proj):
    sources, slot_count, slot_depth, model_width = inbound.shape
    per_source = slot_count * slot_depth
    upper_bound = max(1, 1024 // per_source)
    power_two = 1 << upper_bound.bit_length() - 1
    group_size = math.gcd(sources, power_two)
    stacked = inbound.reshape(
        sources // group_size, group_size, slot_count, slot_depth, model_width
    )
    hidden_units = down_proj.shape[1]

    def apply_block(block_part):
        both_parts = jnp.einsum(
            "bjmd,jdf->bjmf", block_part, gate_up, preferred_element_type=jnp.float32
        )
        activated = (
            jax.nn.silu(both_parts[..., :hidden_units]) * both_parts[..., hidden_units:]
        ).astype(jnp.bfloat16)
        return jnp.einsum(
            "bjmf,jfd->bjmd", activated, down_proj, preferred_element_type=jnp.float32
        ).astype(jnp.bfloat16)

    return lax.map(apply_block, stacked).reshape(inbound.shape)


def body(
    head_outputs,
    residual,
    output_weight,
    router,
    norm_gain,
    placed_gate_up,
    placed_down,
    routes,
    replica_pick,
    placement,
    final_gain,
):
    row_count, model_width = residual.shape
    route_count = routes.shape[1]
    experts = router.shape[1]
    place_count = placement.shape[0]
    groups = lax.axis_size("expert")
    slot_count = place_count // groups
    capacity = CAP
    projected = jnp.dot(
        head_outputs,
        lax.all_gather(output_weight, "shard", axis=0, tiled=True),
        preferred_element_type=jnp.float32,
    )
    hidden = (residual.astype(jnp.float32) + projected).astype(jnp.bfloat16)
    hidden_wide = hidden.astype(jnp.float32)
    normed = rms_scale(hidden_wide, norm_gain).astype(jnp.bfloat16)
    logits = jnp.dot(normed, router, preferred_element_type=jnp.float32)
    labels = jnp.arange(experts, dtype=jnp.int32)
    selector = (routes[..., None] == labels).astype(jnp.float32)
    chosen_logits = jnp.sum(selector * logits[:, None, :], axis=-1)
    raised = jnp.exp(chosen_logits)
    route_weight = raised / jnp.sum(raised, axis=-1, keepdims=True)
    slot_ids = choose_slots(routes, replica_pick, placement, experts).reshape(-1)
    slot_hits = (slot_ids[:, None] == jnp.arange(place_count, dtype=jnp.int32)).astype(jnp.int32)
    slot_rank = jnp.sum((jnp.cumsum(slot_hits, axis=0) - slot_hits) * slot_hits, axis=1)
    copies_out = jnp.repeat(normed, route_count, axis=0)
    gate_up, down_proj = (
        lax.all_gather(placed_gate_up, "shard", axis=1, tiled=True),
        lax.all_gather(placed_down, "shard", axis=1, tiled=True),
    )
    buffer_index = slot_ids * capacity + slot_rank
    outbound = (
        jnp.zeros((place_count * capacity, model_width), jnp.bfloat16)
        .at[buffer_index]
        .set(copies_out)
    )
    inbound = lax.all_to_all(
        outbound.reshape(groups, slot_count * capacity, model_width),
        "expert",
        split_axis=0,
        concat_axis=0,
        tiled=True,
    )
    inbound = inbound.reshape(groups, slot_count, capacity, model_width)
    answers = padded_experts(inbound, gate_up, down_proj)
    returned = lax.all_to_all(
        answers.reshape(groups, slot_count * capacity, model_width),
        "expert",
        split_axis=0,
        concat_axis=0,
        tiled=True,
    )
    returned = returned.reshape(place_count * capacity, model_width)
    gathered = returned[buffer_index].reshape(row_count, route_count, model_width)
    mixture = jnp.sum(route_weight[..., None] * gathered.astype(jnp.float32), axis=1)
    return rms_scale(hidden_wide + mixture, final_gain).astype(jnp.bfloat16)


def solution(mesh):
    return jax.shard_map(
        body,
        mesh=mesh,
        in_specs=(
            P(("expert", "shard"), None),
            P(("expert", "shard"), None),
            P("shard", None),
            P(),
            P(),
            P("expert", "shard", None),
            P("expert", "shard", None),
            P(("expert", "shard"), None),
            P(("expert", "shard"), None),
            P(),
            P(),
        ),
        out_specs=P(("expert", "shard"), None),
        check_vma=False,
    )
```

profile of v0, /device:TPU:8, one launch (start us, length us, event | category | flops | bytes accessed | tf_op | source)
XLA Modules:
  0.0 298.7 jit_solution(8808641445974317560)
XLA Ops:
  12.6 18.0 %reduce-window.6 = s32[64,8,128]{2,1,0:T(8,128)S(1)} reduce-window(s32[64,8,128]{2,1,0:T(8,128)S(1)} %fusion.27, s32[]{:T(128)} %copy.53), window={size=1x1x128 pad=0_0x0_0x127_0}, to_apply=%region_12.13 | reduce-window | flops 8323072 | bytes 524292 | tf_op jit(solution)/shard_map/reduce-window
  31.3 21.6 %all-gather.4.cloned.1.call-done = bf16[1024,1024]{1,0:T(8,128)(2,1)} async-done(((bf16[128,1024]{1,0:T(8,128)(2,1)}), bf16[1024,1024]{1,0:T(8,128)(2,1)}) %all-gather.4.cloned.1.call-update) | async-done | bytes 2097168 | tf_op jit(solution)/shard_map/all_gather | solution.py:83
  52.9 2.1 multiply_reduce_fusion.1
  55.2 9.0 %scatter_custom_fusion = bf16[3072,1024]{1,0:T(8,128)(2,1)} fusion(s32[1024]{0:T(1024)S(1)} %bitcast.75, bf16[]{:T(256)} %constant.52.clone.1, bf16[128,1024]{1,0:T(8,128)(2,1)S(1)} %multiply_convert_fusion.1), kind=kCustom, calls=%fused_computation.18 | custom fusion | bytes 6553602 | tf_op jit(solution)/shard_map/scatter | solution.py:107
  64.2 8.2 %all-to-all-start = ((bf16[32,96,1024]{2,1,0:T(8,128)(2,1)}), bf16[32,96,1024]{2,1,0:T(8,128)(2,1)}, u32[]{:S(2)}, u32[]{:S(2)}) async-start(bf16[32,96,1024]{2,1,0:T(8,128)(2,1)} %bitcast.70), calls=%async_computation | async-start | bytes 12582912 | tf_op jit(solution)/shard_map/all_to_all | solution.py:109
  72.4 22.6 %all-gather.8.cloned.1.call-done = bf16[2,512,1024]{2,1,0:T(8,128)(2,1)} async-done(((bf16[2,64,1024]{2,1,0:T(8,128)(2,1)}), bf16[2,512,1024]{2,1,0:T(8,128)(2,1)}) %all-gather.8.cloned.1.call-update) | async-done | bytes 2097168 | tf_op jit(solution)/shard_map/all_gather | solution.py:101
  95.0 55.0 %all-gather.6.cloned.1.call-done = bf16[2,1024,1024]{2,1,0:T(8,128)(2,1)} async-done(((bf16[2,128,1024]{2,1,0:T(8,128)(2,1)}), bf16[2,1024,1024]{2,1,0:T(8,128)(2,1)}) %all-gather.6.cloned.1.call-update) | async-done | bytes 4194320 | tf_op jit(solution)/shard_map/all_gather | solution.py:100
  150.1 9.9 %all-to-all-done = bf16[32,96,1024]{2,1,0:T(8,128)(2,1)} async-done(((bf16[32,96,1024]{2,1,0:T(8,128)(2,1)}), bf16[32,96,1024]{2,1,0:T(8,128)(2,1)}, u32[]{:S(2)}, u32[]{:S(2)}) %all-to-all-start) | async-done | bytes 6291488 | tf_op jit(solution)/shard_map/all_to_all | solution.py:109
  160.0 27.9 %while.10 = (s32[]{:T(128)}, bf16[4,8,2,48,1024]{4,3,2,1,0:T(8,128)(2,1)}, bf16[4,8,2,48,1024]{4,3,2,1,0:T(8,128)(2,1)}, bf16[2,1024,1024]{2,1,0:T(8,128)(2,1)}, bf16[2,512,1024]{2,1,0:T(8,128)(2,1)}, /*index=5*/s32[]{:T(128)}) while((s32[]{:T(128)}, bf16[4,8,2,48,1024]{4,3,2,1,0:T(8,128)(2,1)}, bf16[4,8,2,48,1024]{4,3,2,1,0:T(8,128)(2,1)}, ...), condition=%wide.region_17.18_spmd, body=%wide.region_16.17_spmd.sunk | while | flops 2419064832 | bytes 27263088 | solution.py:58
  160.0 4.6 %fusion.48 = f32[8,2,48,1024]{3,2,0,1:T(8,128)S(1)} fusion(bf16[2,1024,1024]{2,1,0:T(8,128)(2,1)} %get-tuple-element.113, bf16[4,8,2,48,1024]{4,3,2,1,0:T(8,128)(2,1)} %get-tuple-element.112, s32[]{:T(128)S(6)} %copy.48), kind=kOutput, calls=%fused_computation.6.clone.1 | convolution fusion | flops 1610612736 | bytes 8912900 | tf_op jit(solution)/shard_map/while/body/eval_jaxpr/bjmd,jdf->bjmf/dot_general | solution.py:48
  164.6 1.0 fusion.49
  165.6 1.3 copy_dynamic-update-slice_fusion.2
  166.9 4.6 %fusion.48 = f32[8,2,48,1024]{3,2,0,1:T(8,128)S(1)} fusion(bf16[2,1024,1024]{2,1,0:T(8,128)(2,1)} %get-tuple-element.113, bf16[4,8,2,48,1024]{4,3,2,1,0:T(8,128)(2,1)} %get-tuple-element.112, s32[]{:T(128)S(6)} %copy.48), kind=kOutput, calls=%fused_computation.6.clone.1 | convolution fusion | flops 1610612736 | bytes 8912900 | tf_op jit(solution)/shard_map/while/body/eval_jaxpr/bjmd,jdf->bjmf/dot_general | solution.py:48
  171.6 1.0 fusion.49
  172.6 1.4 copy_dynamic-update-slice_fusion.2
  174.0 4.6 %fusion.48 = f32[8,2,48,1024]{3,2,0,1:T(8,128)S(1)} fusion(bf16[2,1024,1024]{2,1,0:T(8,128)(2,1)} %get-tuple-element.113, bf16[4,8,2,48,1024]{4,3,2,1,0:T(8,128)(2,1)} %get-tuple-element.112, s32[]{:T(128)S(6)} %copy.48), kind=kOutput, calls=%fused_computation.6.clone.1 | convolution fusion | flops 1610612736 | bytes 8912900 | tf_op jit(solution)/shard_map/while/body/eval_jaxpr/bjmd,jdf->bjmf/dot_general | solution.py:48
  178.6 1.0 fusion.49
  179.7 1.3 copy_dynamic-update-slice_fusion.2
  181.0 4.6 %fusion.48 = f32[8,2,48,1024]{3,2,0,1:T(8,128)S(1)} fusion(bf16[2,1024,1024]{2,1,0:T(8,128)(2,1)} %get-tuple-element.113, bf16[4,8,2,48,1024]{4,3,2,1,0:T(8,128)(2,1)} %get-tuple-element.112, s32[]{:T(128)S(6)} %copy.48), kind=kOutput, calls=%fused_computation.6.clone.1 | convolution fusion | flops 1610612736 | bytes 8912900 | tf_op jit(solution)/shard_map/while/body/eval_jaxpr/bjmd,jdf->bjmf/dot_general | solution.py:48
  186.6 1.3 copy_dynamic-update-slice_fusion.2
  187.9 5.1 %all-to-all-start.1 = ((bf16[32,96,1024]{2,1,0:T(8,128)(2,1)}), bf16[32,96,1024]{2,1,0:T(8,128)(2,1)}, u32[]{:S(2)}, u32[]{:S(2)}) async-start(bf16[32,96,1024]{2,1,0:T(8,128)(2,1)} %bitcast.71), calls=%async_computation.1 | async-start | bytes 12582912 | tf_op jit(solution)/shard_map/all_to_all | solution.py:118
  193.5 87.8 %all-to-all-done.1 = bf16[32,96,1024]{2,1,0:T(8,128)(2,1)} async-done(((bf16[32,96,1024]{2,1,0:T(8,128)(2,1)}), bf16[32,96,1024]{2,1,0:T(8,128)(2,1)}, u32[]{:S(2)}, u32[]{:S(2)}) %all-to-all-start.1) | async-done | bytes 6291488 | tf_op jit(solution)/shard_map/all_to_all | solution.py:118
  281.3 8.6 %gather_fusion = bf16[1024,1024]{1,0:T(8,128)(2,1)S(1)} fusion(bf16[3072,1024]{1,0:T(8,128)(2,1)} %bitcast.16, s32[1024]{0:T(1024)S(1)} %broadcast_clamp_fusion), kind=kCustom, calls=%fused_computation | custom fusion | bytes 4198400 | tf_op jit(solution)/shard_map/gather | solution.py:126
  289.9 1.3 fusion.17
  (58 shorter events, 9.2 us)
Async XLA Ops:
  6.5 46.4 %copy-start = (bf16[128,1024]{1,0:T(8,128)(2,1)S(1)}, bf16[128,1024]{1,0:T(8,128)(2,1)}, u32[]{:S(2)}) copy-start(bf16[128,1024]{1,0:T(8,128)(2,1)} %param.13) | copy-start | bytes 786436
  6.5 46.4 %copy-start.1 = (bf16[128,1024]{1,0:T(8,128)(2,1)S(1)}, bf16[128,1024]{1,0:T(8,128)(2,1)}, u32[]{:S(2)}) copy-start(bf16[128,1024]{1,0:T(8,128)(2,1)} %param.14) | copy-start | bytes 786436
  6.5 46.4 %all-gather.4.cloned.1.call-start = ((), (), s32[]{:S(2)}) async-start(), calls=%async_computation.2 | async-start | bytes 2359296 | tf_op jit(solution)/shard_map/all_gather | solution.py:83
  7.3 87.8 %all-gather.8.cloned.1.call-start = ((), (), s32[]{:S(2)}) async-start(), calls=%async_computation.4 | async-start | bytes 2359296 | tf_op jit(solution)/shard_map/all_gather | solution.py:101
  8.0 142.1 %all-gather.6.cloned.1.call-start = ((), (), s32[]{:S(2)}) async-start(), calls=%async_computation.3 | async-start | bytes 4718592 | tf_op jit(solution)/shard_map/all_gather | solution.py:100
  30.7 24.3 %copy-start.4 = (f32[1024]{0:T(1024)S(1)}, f32[1024]{0:T(1024)}, u32[]{:S(2)}) copy-start(f32[1024]{0:T(1024)} %param.17) | copy-start | bytes 12292
  64.2 95.8 %all-to-all-start = ((bf16[32,96,1024]{2,1,0:T(8,128)(2,1)}), bf16[32,96,1024]{2,1,0:T(8,128)(2,1)}, u32[]{:S(2)}, u32[]{:S(2)}) async-start(bf16[32,96,1024]{2,1,0:T(8,128)(2,1)} %bitcast.70), calls=%async_computation | async-start | bytes 12582912 | tf_op jit(solution)/shard_map/all_to_all | solution.py:109
  160.0 4.6 %copy-start.6 = (bf16[2,512,1024]{2,1,0:T(8,128)(2,1)S(1)}, bf16[2,512,1024]{2,1,0:T(8,128)(2,1)}, u32[]{:S(2)}) copy-start(bf16[2,512,1024]{2,1,0:T(8,128)(2,1)} %get-tuple-element.114) | copy-start | bytes 6291460 | tf_op jit(solution)/shard_map/while
  166.9 4.6 %copy-start.6 = (bf16[2,512,1024]{2,1,0:T(8,128)(2,1)S(1)}, bf16[2,512,1024]{2,1,0:T(8,128)(2,1)}, u32[]{:S(2)}) copy-start(bf16[2,512,1024]{2,1,0:T(8,128)(2,1)} %get-tuple-element.114) | copy-start | bytes 6291460 | tf_op jit(solution)/shard_map/while
  174.0 4.6 %copy-start.6 = (bf16[2,512,1024]{2,1,0:T(8,128)(2,1)S(1)}, bf16[2,512,1024]{2,1,0:T(8,128)(2,1)}, u32[]{:S(2)}) copy-start(bf16[2,512,1024]{2,1,0:T(8,128)(2,1)} %get-tuple-element.114) | copy-start | bytes 6291460 | tf_op jit(solution)/shard_map/while
  181.0 4.6 %copy-start.6 = (bf16[2,512,1024]{2,1,0:T(8,128)(2,1)S(1)}, bf16[2,512,1024]{2,1,0:T(8,128)(2,1)}, u32[]{:S(2)}) copy-start(bf16[2,512,1024]{2,1,0:T(8,128)(2,1)} %get-tuple-element.114) | copy-start | bytes 6291460 | tf_op jit(solution)/shard_map/while
  187.9 5.1 %copy-start.2 = (bf16[1024,32]{0,1:T(8,128)(2,1)S(1)}, bf16[1024,32]{0,1:T(8,128)(2,1)}, u32[]{:S(2)}) copy-start(bf16[1024,32]{0,1:T(8,128)(2,1)} %param.16) | copy-start | bytes 196612
  187.9 5.3 %copy-start.3 = (s32[128,8]{0,1:T(8,128)S(1)}, s32[128,8]{0,1:T(8,128)}, u32[]{:S(2)}) copy-start(s32[128,8]{0,1:T(8,128)} %param.20) | copy-start | bytes 12292
  187.9 93.4 %all-to-all-start.1 = ((bf16[32,96,1024]{2,1,0:T(8,128)(2,1)}), bf16[32,96,1024]{2,1,0:T(8,128)(2,1)}, u32[]{:S(2)}, u32[]{:S(2)}) async-start(bf16[32,96,1024]{2,1,0:T(8,128)(2,1)} %bitcast.71), calls=%async_computation.1 | async-start | bytes 12582912 | tf_op jit(solution)/shard_map/all_to_all | solution.py:118
  289.9 1.5 copy-start.5
Sparse Core Ops, SparseCore 0:
  9.2 43.6 all-gather.3
  54.7 40.2 all-gather.7
  96.8 53.1 all-gather.5
where the time goes:
time: 299 us
  waiting for transfers between devices  199 us (67%)
  matrix products  24.8 us (8%)
  other arithmetic  24.1 us (8%)
  local copies, waits for them, and re-layouts  23.9 us (8%)
  starting transfers between devices  13.4 us (4%)
  between operations  13.3 us (4%)
    all_to_all x1, waiting for transfers between devices, body(): lax.all_to_all(answers.reshape(groups, slot_count * capacity, model_width...  87.8 us
    all_gather x1, waiting for transfers between devices, body(): lax.all_gather(placed_gate_up, 'shard', axis=1, tiled=True)  55 us
    all_gather x1, waiting for transfers between devices, body(): lax.all_gather(placed_down, 'shard', axis=1, tiled=True)  22.6 us
    all_gather x1, waiting for transfers between devices, body(): lax.all_gather(output_weight, 'shard', axis=0, tiled=True)  21.6 us
    dot_general x4, matrix products, apply_block(): jnp.einsum('bjmd,jdf->bjmf', block_part, gate_up, preferred_element_type=...  18.4 us
    another operation x3, other arithmetic  18.2 us
    all_to_all x1, waiting for transfers between devices, body(): lax.all_to_all(outbound.reshape(groups, slot_count * capacity, model_widt...  9.92 us
    scatter x1, local copies, waits for them, and re-layouts, body(): outbound = jnp.zeros((place_count * capacity, model_width), jnp.bfloat16)...  9.04 us
  transfers between devices with their start and end apart: 5, of which 5 were waited for; matrix products, arithmetic and copies ran while one was open for 11% of the time, Pallas kernels for 0%

commit v1 on v0

--- a/solution.py
+++ b/solution.py
@@ -97,7 +97,10 @@
     slot_rank = jnp.sum((jnp.cumsum(slot_hits, axis=0) - slot_hits) * slot_hits, axis=1)
     copies_out = jnp.repeat(normed, route_count, axis=0)
     gate_up, down_proj = (
-        lax.all_gather(placed_gate_up, "shard", axis=1, tiled=True),
+        jnp.concatenate(
+            lax.all_to_all(jnp.stack([placed_gate_up] * lax.axis_size("shard")), "shard", 0, 0),
+            axis=1,
+        ),
         lax.all_gather(placed_down, "shard", axis=1, tiled=True),
     )
     buffer_index = slot_ids * capacity + slot_rank

time: 299 us -> 369 us (1.23)
  waiting for transfers between devices: 199 us -> 255 us
  local copies, waits for them, and re-layouts: 23.9 us -> 32.3 us
  starting transfers between devices: 13.4 us -> 21.4 us
    all_gather x1 -> x0, waiting for transfers between devices: 55 us -> none  [body(): lax.all_gather(placed_gate_up, 'shard', axis=1, tiled=True)]
    all_gather x1, waiting for transfers between devices: 21.6 us -> 68.6 us  [body(): lax.all_gather(output_weight, 'shard', axis=0, tiled=True)]
    all_to_all x1, waiting for transfers between devices: 9.92 us -> 47.5 us  [body(): lax.all_to_all(outbound.reshape(groups, slot_count * capacity, model_widt...]
    all_to_all x0 -> x1, waiting for transfers between devices: none -> 15.4 us  [body(): lax.all_to_all(jnp.stack([placed_gate_up] * lax.axis_size('shard')), 'sha...]
    all_gather x1, waiting for transfers between devices: 22.6 us -> 34.5 us  [body(): lax.all_gather(placed_down, 'shard', axis=1, tiled=True)]
    all_to_all x0 -> x1, starting transfers between devices: none -> 8.6 us  [body(): lax.all_to_all(jnp.stack([placed_gate_up] * lax.axis_size('shard')), 'sha...]
    all_to_all x0 -> x1, local copies, waits for them, and re-layouts: none -> 4.82 us  [body(): lax.all_to_all(jnp.stack([placed_gate_up] * lax.axis_size('shard')), 'sha...]
  transfers between devices with their start and end apart: 5 -> 5, of which waited for: 5 -> 5; matrix products, arithmetic and copies ran while one was open for 11% -> 10% of each run, Pallas kernels for 0% -> 0%
where the time goes in v1:
time: 369 us
  waiting for transfers between devices  255 us (69%)
  local copies, waits for them, and re-layouts  32.3 us (9%)
  matrix products  24.8 us (7%)
  starting transfers between devices  21.4 us (6%)
  other arithmetic  21.4 us (6%)
  between operations  13.6 us (4%)
    all_to_all x1, waiting for transfers between devices, body(): lax.all_to_all(answers.reshape(groups, slot_count * capacity, model_width...  87.8 us
    all_gather x1, waiting for transfers between devices, body(): lax.all_gather(output_weight, 'shard', axis=0, tiled=True)  68.6 us
    all_to_all x1, waiting for transfers between devices, body(): lax.all_to_all(outbound.reshape(groups, slot_count * capacity, model_widt...  47.5 us
    all_gather x1, waiting for transfers between devices, body(): lax.all_gather(placed_down, 'shard', axis=1, tiled=True)  34.5 us
    dot_general x4, matrix products, apply_block(): jnp.einsum('bjmd,jdf->bjmf', block_part, gate_up, preferred_element_type=...  18.4 us
    another operation x3, other arithmetic  18.2 us
    all_to_all x1, waiting for transfers between devices, body(): lax.all_to_all(jnp.stack([placed_gate_up] * lax.axis_size('shard')), 'sha...  15.4 us
    scatter x1, local copies, waits for them, and re-layouts, body(): outbound = jnp.zeros((place_count * capacity, model_width), jnp.bfloat16)...  9.08 us
  transfers between devices with their start and end apart: 5, of which 5 were waited for; matrix products, arithmetic and copies ran while one was open for 10% of the time, Pallas kernels for 0%

profile of v1, /device:TPU:8, one launch (start us, length us, event | category | flops | bytes accessed | tf_op | source)
XLA Modules:
  0.0 368.8 jit_solution(10193764956387213659)
XLA Ops:
  6.5 3.5 stack.2
  10.1 8.6 %all-to-all-start.1 = ((bf16[8,2,128,1024]{3,2,1,0:T(8,128)(2,1)}), bf16[8,2,128,1024]{3,2,1,0:T(8,128)(2,1)}, u32[]{:S(2)}, u32[]{:S(2)}) async-start(bf16[8,2,128,1024]{3,2,1,0:T(8,128)(2,1)} %stack.2), calls=%async_computation.1 | async-start | bytes 8388608 | tf_op jit(solution)/shard_map/all_to_all | solution.py:101
  20.6 18.0 %reduce-window.6 = s32[64,8,128]{2,1,0:T(8,128)S(1)} reduce-window(s32[64,8,128]{2,1,0:T(8,128)S(1)} %fusion.27, s32[]{:T(128)} %copy.73), window={size=1x1x128 pad=0_0x0_0x127_0}, to_apply=%region_12.13 | reduce-window | flops 8323072 | bytes 524292 | tf_op jit(solution)/shard_map/reduce-window
  39.3 68.6 %all-gather.3.cloned.1.call-done = bf16[1024,1024]{1,0:T(8,128)(2,1)} async-done(((bf16[128,1024]{1,0:T(8,128)(2,1)}), bf16[1024,1024]{1,0:T(8,128)(2,1)}) %all-gather.3.cloned.1.call-update) | async-done | bytes 2097168 | tf_op jit(solution)/shard_map/all_gather | solution.py:83
  107.9 2.1 multiply_reduce_fusion.1
  110.1 9.1 %scatter_custom_fusion = bf16[3072,1024]{1,0:T(8,128)(2,1)} fusion(s32[1024]{0:T(1024)S(1)} %bitcast.79, bf16[]{:T(256)} %constant.52.clone.1, bf16[128,1024]{1,0:T(8,128)(2,1)S(1)} %multiply_convert_fusion.1), kind=kCustom, calls=%fused_computation.18 | custom fusion | bytes 6553602 | tf_op jit(solution)/shard_map/scatter | solution.py:110
  119.2 15.4 %all-to-all-done.1 = bf16[8,2,128,1024]{3,2,1,0:T(8,128)(2,1)} async-done(((bf16[8,2,128,1024]{3,2,1,0:T(8,128)(2,1)}), bf16[8,2,128,1024]{3,2,1,0:T(8,128)(2,1)}, u32[]{:S(2)}, u32[]{:S(2)}) %all-to-all-start.1) | async-done | bytes 4194336 | tf_op jit(solution)/shard_map/all_to_all | solution.py:101
  134.6 7.6 %all-to-all-start = ((bf16[32,96,1024]{2,1,0:T(8,128)(2,1)}), bf16[32,96,1024]{2,1,0:T(8,128)(2,1)}, u32[]{:S(2)}, u32[]{:S(2)}) async-start(bf16[32,96,1024]{2,1,0:T(8,128)(2,1)} %bitcast.73), calls=%async_computation | async-start | bytes 12582912 | tf_op jit(solution)/shard_map/all_to_all | solution.py:112
  143.0 4.8 %copy.48 = bf16[8,2,128,1024]{3,2,0,1:T(8,128)(2,1)} copy(bf16[8,2,128,1024]{3,2,1,0:T(8,128)(2,1)} %all-to-all-done.1) | data formatting | bytes 8388608 | tf_op jit(solution)/shard_map/all_to_all | solution.py:101
  147.8 34.5 %all-gather.5.cloned.1.call-done = bf16[2,512,1024]{2,1,0:T(8,128)(2,1)} async-done(((bf16[2,64,1024]{2,1,0:T(8,128)(2,1)}), bf16[2,512,1024]{2,1,0:T(8,128)(2,1)}) %all-gather.5.cloned.1.call-update) | async-done | bytes 2097168 | tf_op jit(solution)/shard_map/all_gather | solution.py:104
  182.3 47.5 %all-to-all-done = bf16[32,96,1024]{2,1,0:T(8,128)(2,1)} async-done(((bf16[32,96,1024]{2,1,0:T(8,128)(2,1)}), bf16[32,96,1024]{2,1,0:T(8,128)(2,1)}, u32[]{:S(2)}, u32[]{:S(2)}) %all-to-all-start) | async-done | bytes 6291488 | tf_op jit(solution)/shard_map/all_to_all | solution.py:112
  229.8 27.9 %while.10 = (s32[]{:T(128)}, bf16[4,8,2,48,1024]{4,3,2,1,0:T(8,128)(2,1)}, bf16[4,8,2,48,1024]{4,3,2,1,0:T(8,128)(2,1)}, bf16[2,1024,1024]{2,1,0:T(8,128)(2,1)}, bf16[2,512,1024]{2,1,0:T(8,128)(2,1)}, /*index=5*/s32[]{:T(128)}) while((s32[]{:T(128)}, bf16[4,8,2,48,1024]{4,3,2,1,0:T(8,128)(2,1)}, bf16[4,8,2,48,1024]{4,3,2,1,0:T(8,128)(2,1)}, ...), condition=%wide.region_17.18_spmd, body=%wide.region_16.17_spmd.sunk | while | flops 2419064832 | bytes 27263088 | solution.py:58
  229.8 4.6 %fusion.48 = f32[8,2,48,1024]{3,2,0,1:T(8,128)S(1)} fusion(bf16[2,1024,1024]{2,1,0:T(8,128)(2,1)} %get-tuple-element.123, bf16[4,8,2,48,1024]{4,3,2,1,0:T(8,128)(2,1)} %get-tuple-element.122, s32[]{:T(128)S(6)} %copy.68), kind=kOutput, calls=%fused_computation.6.clone.1 | convolution fusion | flops 1610612736 | bytes 8912900 | tf_op jit(solution)/shard_map/while/body/eval_jaxpr/bjmd,jdf->bjmf/dot_general | solution.py:48
  235.5 1.4 copy_dynamic-update-slice_fusion.2
  236.8 4.6 %fusion.48 = f32[8,2,48,1024]{3,2,0,1:T(8,128)S(1)} fusion(bf16[2,1024,1024]{2,1,0:T(8,128)(2,1)} %get-tuple-element.123, bf16[4,8,2,48,1024]{4,3,2,1,0:T(8,128)(2,1)} %get-tuple-element.122, s32[]{:T(128)S(6)} %copy.68), kind=kOutput, calls=%fused_computation.6.clone.1 | convolution fusion | flops 1610612736 | bytes 8912900 | tf_op jit(solution)/shard_map/while/body/eval_jaxpr/bjmd,jdf->bjmf/dot_general | solution.py:48
  242.5 1.3 copy_dynamic-update-slice_fusion.2
  243.8 4.6 %fusion.48 = f32[8,2,48,1024]{3,2,0,1:T(8,128)S(1)} fusion(bf16[2,1024,1024]{2,1,0:T(8,128)(2,1)} %get-tuple-element.123, bf16[4,8,2,48,1024]{4,3,2,1,0:T(8,128)(2,1)} %get-tuple-element.122, s32[]{:T(128)S(6)} %copy.68), kind=kOutput, calls=%fused_computation.6.clone.1 | convolution fusion | flops 1610612736 | bytes 8912900 | tf_op jit(solution)/shard_map/while/body/eval_jaxpr/bjmd,jdf->bjmf/dot_general | solution.py:48
  249.4 1.3 copy_dynamic-update-slice_fusion.2
  250.7 4.6 %fusion.48 = f32[8,2,48,1024]{3,2,0,1:T(8,128)S(1)} fusion(bf16[2,1024,1024]{2,1,0:T(8,128)(2,1)} %get-tuple-element.123, bf16[4,8,2,48,1024]{4,3,2,1,0:T(8,128)(2,1)} %get-tuple-element.122, s32[]{:T(128)S(6)} %copy.68), kind=kOutput, calls=%fused_computation.6.clone.1 | convolution fusion | flops 1610612736 | bytes 8912900 | tf_op jit(solution)/shard_map/while/body/eval_jaxpr/bjmd,jdf->bjmf/dot_general | solution.py:48
  256.4 1.4 copy_dynamic-update-slice_fusion.2
  257.7 5.1 %all-to-all-start.2 = ((bf16[32,96,1024]{2,1,0:T(8,128)(2,1)}), bf16[32,96,1024]{2,1,0:T(8,128)(2,1)}, u32[]{:S(2)}, u32[]{:S(2)}) async-start(bf16[32,96,1024]{2,1,0:T(8,128)(2,1)} %bitcast.74), calls=%async_computation.2 | async-start | bytes 12582912 | tf_op jit(solution)/shard_map/all_to_all | solution.py:121
  263.3 87.8 %all-to-all-done.2 = bf16[32,96,1024]{2,1,0:T(8,128)(2,1)} async-done(((bf16[32,96,1024]{2,1,0:T(8,128)(2,1)}), bf16[32,96,1024]{2,1,0:T(8,128)(2,1)}, u32[]{:S(2)}, u32[]{:S(2)}) %all-to-all-start.2) | async-done | bytes 6291488 | tf_op jit(solution)/shard_map/all_to_all | solution.py:121
  351.1 8.6 %gather_fusion = bf16[1024,1024]{1,0:T(8,128)(2,1)S(1)} fusion(bf16[3072,1024]{1,0:T(8,128)(2,1)} %bitcast.18, s32[1024]{0:T(1024)S(1)} %broadcast_clamp_fusion), kind=kCustom, calls=%fused_computation | custom fusion | bytes 4198400 | tf_op jit(solution)/shard_map/gather | solution.py:129
  359.7 1.3 fusion.17
  (63 shorter events, 8.9 us)
Async XLA Ops:
  6.5 101.3 %copy-start = (bf16[128,1024]{1,0:T(8,128)(2,1)S(1)}, bf16[128,1024]{1,0:T(8,128)(2,1)}, u32[]{:S(2)}) copy-start(bf16[128,1024]{1,0:T(8,128)(2,1)} %param.13) | copy-start | bytes 786436
  10.1 9.3 %copy-start.7 = (s32[64]{0:T(128)S(1)}, s32[64]{0:T(128)}, u32[]{:S(2)}) copy-start(s32[64]{0:T(128)} %param.22) | copy-start | bytes 772
  10.1 9.7 %copy-start.3 = (s32[128,8]{0,1:T(8,128)S(1)}, s32[128,8]{0,1:T(8,128)}, u32[]{:S(2)}) copy-start(s32[128,8]{0,1:T(8,128)} %param.20) | copy-start | bytes 12292
  10.1 9.9 %copy-start.6 = (s32[128,8]{0,1:T(8,128)S(1)}, s32[128,8]{0,1:T(8,128)}, u32[]{:S(2)}) copy-start(s32[128,8]{0,1:T(8,128)} %param.21) | copy-start | bytes 12292
  10.1 124.5 %all-to-all-start.1 = ((bf16[8,2,128,1024]{3,2,1,0:T(8,128)(2,1)}), bf16[8,2,128,1024]{3,2,1,0:T(8,128)(2,1)}, u32[]{:S(2)}, u32[]{:S(2)}) async-start(bf16[8,2,128,1024]{3,2,1,0:T(8,128)(2,1)} %stack.2), calls=%async_computation.1 | async-start | bytes 8388608 | tf_op jit(solution)/shard_map/all_to_all | solution.py:101
  18.7 89.2 %copy-start.1 = (bf16[128,1024]{1,0:T(8,128)(2,1)S(1)}, bf16[128,1024]{1,0:T(8,128)(2,1)}, u32[]{:S(2)}) copy-start(bf16[128,1024]{1,0:T(8,128)(2,1)} %param.14) | copy-start | bytes 786436
  18.7 89.2 %all-gather.3.cloned.1.call-start = ((), (), s32[]{:S(2)}) async-start(), calls=%async_computation.3 | async-start | bytes 2359296 | tf_op jit(solution)/shard_map/all_gather | solution.py:83
  38.8 71.2 %copy-start.4 = (f32[1024]{0:T(1024)S(1)}, f32[1024]{0:T(1024)}, u32[]{:S(2)}) copy-start(f32[1024]{0:T(1024)} %param.17) | copy-start | bytes 12292
  134.6 95.2 %all-to-all-start = ((bf16[32,96,1024]{2,1,0:T(8,128)(2,1)}), bf16[32,96,1024]{2,1,0:T(8,128)(2,1)}, u32[]{:S(2)}, u32[]{:S(2)}) async-start(bf16[32,96,1024]{2,1,0:T(8,128)(2,1)} %bitcast.73), calls=%async_computation | async-start | bytes 12582912 | tf_op jit(solution)/shard_map/all_to_all | solution.py:112
  142.2 40.0 %all-gather.5.cloned.1.call-start = ((), (), s32[]{:S(2)}) async-start(), calls=%async_computation.4 | async-start | bytes 2359296 | tf_op jit(solution)/shard_map/all_gather | solution.py:104
  229.8 4.6 %copy-start.8 = (bf16[2,512,1024]{2,1,0:T(8,128)(2,1)S(1)}, bf16[2,512,1024]{2,1,0:T(8,128)(2,1)}, u32[]{:S(2)}) copy-start(bf16[2,512,1024]{2,1,0:T(8,128)(2,1)} %get-tuple-element.124) | copy-start | bytes 6291460 | tf_op jit(solution)/shard_map/while
  236.8 4.6 %copy-start.8 = (bf16[2,512,1024]{2,1,0:T(8,128)(2,1)S(1)}, bf16[2,512,1024]{2,1,0:T(8,128)(2,1)}, u32[]{:S(2)}) copy-start(bf16[2,512,1024]{2,1,0:T(8,128)(2,1)} %get-tuple-element.124) | copy-start | bytes 6291460 | tf_op jit(solution)/shard_map/while
  243.8 4.6 %copy-start.8 = (bf16[2,512,1024]{2,1,0:T(8,128)(2,1)S(1)}, bf16[2,512,1024]{2,1,0:T(8,128)(2,1)}, u32[]{:S(2)}) copy-start(bf16[2,512,1024]{2,1,0:T(8,128)(2,1)} %get-tuple-element.124) | copy-start | bytes 6291460 | tf_op jit(solution)/shard_map/while
  250.7 4.6 %copy-start.8 = (bf16[2,512,1024]{2,1,0:T(8,128)(2,1)S(1)}, bf16[2,512,1024]{2,1,0:T(8,128)(2,1)}, u32[]{:S(2)}) copy-start(bf16[2,512,1024]{2,1,0:T(8,128)(2,1)} %get-tuple-element.124) | copy-start | bytes 6291460 | tf_op jit(solution)/shard_map/while
  257.7 5.1 %copy-start.2 = (bf16[1024,32]{0,1:T(8,128)(2,1)S(1)}, bf16[1024,32]{0,1:T(8,128)(2,1)}, u32[]{:S(2)}) copy-start(bf16[1024,32]{0,1:T(8,128)(2,1)} %param.16) | copy-start | bytes 196612
  257.7 93.3 %all-to-all-start.2 = ((bf16[32,96,1024]{2,1,0:T(8,128)(2,1)}), bf16[32,96,1024]{2,1,0:T(8,128)(2,1)}, u32[]{:S(2)}, u32[]{:S(2)}) async-start(bf16[32,96,1024]{2,1,0:T(8,128)(2,1)} %bitcast.74), calls=%async_computation.2 | async-start | bytes 12582912 | tf_op jit(solution)/shard_map/all_to_all | solution.py:121
  359.7 1.5 copy-start.5
Sparse Core Ops, SparseCore 0:
  21.3 86.5 all-gather.2
  144.8 37.3 all-gather.4
